TPU v7x, 128 devices: a whole 4x4x4 slice. The times are simulated.
128 devices in a mesh: col: 16 (over y, x), row: 8 (over z, core).
Axes of the slice: x: 4, y: 4, z: 4, core: 2. Of those that a mesh axis runs over, the one named last changes fastest.
Arguments:
- matrix: float32 [24, 512, 8192], P(None, 'row', 'col'), may hold values from -0.4 to 2.4, as said below
- pivots: int32 [16, 512], replicated, may hold values from 0 to 511, as said below
- seeds: float32 [16, 512, 512], P('col'), may hold values from -1 to 2, as said below
Outputs:
- factors: float32 [24, 512, 8192], P(None, 'row', 'col')
Inputs may be any that keep to these rules, and one draw needn't show every extreme that they name: Each row of pivots is an ordering of 0 .. 511. Block (r, j) of matrix is zero where r and j differ by more than 8. seeds[k] approximates the inverse of block (k, k) of matrix after the replacement of rows by pivots[k].
All inputs are finite; a program needn't handle non-finite values.
Results may differ from a plain program's by a relative error of at most 0.0001.
Values sent between devices are 32-bit elements; how exact they have to be, the bound alone decides.
No kernel may reach another device: no remote copies, remote signals or barrier semaphores. Data moves between devices by JAX's collectives and lax.ppermute only.
A program may use at most 64 MiB of HBM per device.

v0:
```python
import jax
import jax.numpy as jnp
from jax import lax
from jax.sharding import PartitionSpec as P

HB = 8
SWEEPS = 2


def sent_to_all(array, axis):
    length = lax.axis_size(axis)
    return lax.all_to_all(
        jnp.broadcast_to(array[None], (length, *array.shape)), axis, 0, 0, tiled=True
    )


def in_order(parts, dim):
    lengths = list(parts.shape[1:])
    lengths[dim] *= parts.shape[0]
    return jnp.moveaxis(parts, 0, dim).reshape(lengths)


def collect(array, axis, dim):
    parts = sent_to_all(array, axis)
    return in_order(parts, dim)


def from_root(block, axis, source):
    block = jnp.where(lax.axis_index(axis) == source, block, jnp.zeros_like(block))
    return lax.psum(block, axis)


def dot_high(left, right):
    return jnp.dot(left, right, precision=lax.Precision.HIGHEST, preferred_element_type=jnp.float32)


def refine(pivot_block, approx, identity):
    for sweep_index in range(SWEEPS):
        approx = dot_high(approx, 2.0 * identity - dot_high(pivot_block, approx))
    return approx


def local(matrix, pivots, seeds):
    col_count = lax.axis_size("col")
    col_index = lax.axis_index("col")
    row_index = lax.axis_index("row")
    row_share = matrix.shape[1]
    panel_width = matrix.shape[2]
    identity = jnp.eye(panel_width, dtype=jnp.float32)
    seed_block = seeds[0]

    def eliminate(panel_index, factors):
        local_row = lax.dynamic_index_in_dim(factors, panel_index, 0, keepdims=False)
        block_row = collect(local_row, "row", 0)
        ordering = lax.dynamic_index_in_dim(pivots, panel_index, 0, keepdims=False)
        swapped = jnp.take(block_row, ordering, axis=0)
        block_row = jnp.where(col_index >= panel_index, swapped, block_row)
        local_row = lax.dynamic_slice_in_dim(block_row, row_index * row_share, row_share, 0)
        factors = lax.dynamic_update_index_in_dim(factors, local_row, panel_index, 0)
        is_owner = col_index == panel_index
        approx = lax.cond(
            is_owner, lambda: refine(block_row, seed_block, identity), lambda: seed_block
        )
        below_rows = lax.dynamic_slice_in_dim(factors, panel_index + 1, HB, 0)
        below_flat = below_rows.reshape(HB * row_share, panel_width)
        scaled = lax.cond(is_owner, lambda: dot_high(below_flat, approx), lambda: below_flat)
        in_reach = (col_index > panel_index) & (col_index <= panel_index + HB)
        arrived = from_root(scaled, "col", panel_index)
        updated = below_flat - dot_high(arrived, block_row)
        result = jnp.where(is_owner, scaled, jnp.where(in_reach, updated, below_flat))
        return lax.dynamic_update_slice_in_dim(
            factors, result.reshape(HB, row_share, panel_width), panel_index + 1, 0
        )

    return lax.fori_loop(0, col_count, eliminate, matrix)


def solution(mesh):
    return jax.shard_map(
        local,
        mesh=mesh,
        in_specs=(P(None, "row", "col"), P(), P("col", None, None)),
        out_specs=P(None, "row", "col"),
        check_vma=False,
    )
```

profile of v0, /device:TPU:0, one launch (start us, length us, event | category | flops | bytes accessed | tf_op | source)
XLA Modules:
  0.0 2143.6 jit_solution(5086388667008317163)
XLA Ops:
  10.7 2126.4 %while.17 = (s32[]{:T(128)}, f32[24,64,512]{2,1,0:T(8,128)}, s32[]{:T(128)}, s32[16,512]{1,0:T(8,128)}, s32[]{:T(128)}, /*index=5*/f32[512,512]{1,0:T(8,128)S(1)...) while((s32[]{:T(128)}, f32[24,64,512]{2,1,0:T(8,128)}, ...), condition=%wide.region_6.7_spmd.clone.clone, body=%wide.region_0.6_spmd.clone.clone.sunk | while | flops 9667090432 | bytes 55199700 | solution.py:75
  20.0 14.0 all-to-all-done
  57.5 81.4 %all-reduce.2.cloned.1.call-done = f32[512,512]{1,0:T(8,128)} async-done(((f32[512,512]{1,0:T(8,128)}), f32[512,512]{1,0:T(8,128)}) %all-reduce.2.cloned.1.call-update) | async-done | bytes 1048592 | tf_op jit(solution)/shard_map/while/body/eval_jaxpr/psum | solution.py:30
  151.8 14.0 all-to-all-done
  174.7 96.1 %all-reduce.2.cloned.1.call-done = f32[512,512]{1,0:T(8,128)} async-done(((f32[512,512]{1,0:T(8,128)}), f32[512,512]{1,0:T(8,128)}) %all-reduce.2.cloned.1.call-update) | async-done | bytes 1048592 | tf_op jit(solution)/shard_map/while/body/eval_jaxpr/psum | solution.py:30
  283.4 14.0 all-to-all-done
  306.3 97.1 %all-reduce.2.cloned.1.call-done = f32[512,512]{1,0:T(8,128)} async-done(((f32[512,512]{1,0:T(8,128)}), f32[512,512]{1,0:T(8,128)}) %all-reduce.2.cloned.1.call-update) | async-done | bytes 1048592 | tf_op jit(solution)/shard_map/while/body/eval_jaxpr/psum | solution.py:30
  416.0 14.0 all-to-all-done
  438.9 97.7 %all-reduce.2.cloned.1.call-done = f32[512,512]{1,0:T(8,128)} async-done(((f32[512,512]{1,0:T(8,128)}), f32[512,512]{1,0:T(8,128)}) %all-reduce.2.cloned.1.call-update) | async-done | bytes 1048592 | tf_op jit(solution)/shard_map/while/body/eval_jaxpr/psum | solution.py:30
  549.1 14.0 all-to-all-done
  572.1 96.4 %all-reduce.2.cloned.1.call-done = f32[512,512]{1,0:T(8,128)} async-done(((f32[512,512]{1,0:T(8,128)}), f32[512,512]{1,0:T(8,128)}) %all-reduce.2.cloned.1.call-update) | async-done | bytes 1048592 | tf_op jit(solution)/shard_map/while/body/eval_jaxpr/psum | solution.py:30
  681.0 14.0 all-to-all-done
  703.9 96.1 %all-reduce.2.cloned.1.call-done = f32[512,512]{1,0:T(8,128)} async-done(((f32[512,512]{1,0:T(8,128)}), f32[512,512]{1,0:T(8,128)}) %all-reduce.2.cloned.1.call-update) | async-done | bytes 1048592 | tf_op jit(solution)/shard_map/while/body/eval_jaxpr/psum | solution.py:30
  812.6 14.0 all-to-all-done
  835.5 97.3 %all-reduce.2.cloned.1.call-done = f32[512,512]{1,0:T(8,128)} async-done(((f32[512,512]{1,0:T(8,128)}), f32[512,512]{1,0:T(8,128)}) %all-reduce.2.cloned.1.call-update) | async-done | bytes 1048592 | tf_op jit(solution)/shard_map/while/body/eval_jaxpr/psum | solution.py:30
  945.4 14.0 all-to-all-done
  968.3 97.3 %all-reduce.2.cloned.1.call-done = f32[512,512]{1,0:T(8,128)} async-done(((f32[512,512]{1,0:T(8,128)}), f32[512,512]{1,0:T(8,128)}) %all-reduce.2.cloned.1.call-update) | async-done | bytes 1048592 | tf_op jit(solution)/shard_map/while/body/eval_jaxpr/psum | solution.py:30
  1078.2 14.0 all-to-all-done
  1101.1 97.0 %all-reduce.2.cloned.1.call-done = f32[512,512]{1,0:T(8,128)} async-done(((f32[512,512]{1,0:T(8,128)}), f32[512,512]{1,0:T(8,128)}) %all-reduce.2.cloned.1.call-update) | async-done | bytes 1048592 | tf_op jit(solution)/shard_map/while/body/eval_jaxpr/psum | solution.py:30
  1210.7 14.0 all-to-all-done
  1233.6 97.5 %all-reduce.2.cloned.1.call-done = f32[512,512]{1,0:T(8,128)} async-done(((f32[512,512]{1,0:T(8,128)}), f32[512,512]{1,0:T(8,128)}) %all-reduce.2.cloned.1.call-update) | async-done | bytes 1048592 | tf_op jit(solution)/shard_map/while/body/eval_jaxpr/psum | solution.py:30
  1343.6 14.0 all-to-all-done
  1366.5 98.8 %all-reduce.2.cloned.1.call-done = f32[512,512]{1,0:T(8,128)} async-done(((f32[512,512]{1,0:T(8,128)}), f32[512,512]{1,0:T(8,128)}) %all-reduce.2.cloned.1.call-update) | async-done | bytes 1048592 | tf_op jit(solution)/shard_map/while/body/eval_jaxpr/psum | solution.py:30
  1477.9 14.0 all-to-all-done
  1500.8 98.6 %all-reduce.2.cloned.1.call-done = f32[512,512]{1,0:T(8,128)} async-done(((f32[512,512]{1,0:T(8,128)}), f32[512,512]{1,0:T(8,128)}) %all-reduce.2.cloned.1.call-update) | async-done | bytes 1048592 | tf_op jit(solution)/shard_map/while/body/eval_jaxpr/psum | solution.py:30
  1612.0 14.0 all-to-all-done
  1634.9 97.6 %all-reduce.2.cloned.1.call-done = f32[512,512]{1,0:T(8,128)} async-done(((f32[512,512]{1,0:T(8,128)}), f32[512,512]{1,0:T(8,128)}) %all-reduce.2.cloned.1.call-update) | async-done | bytes 1048592 | tf_op jit(solution)/shard_map/while/body/eval_jaxpr/psum | solution.py:30
  1745.1 14.0 all-to-all-done
  1768.0 97.2 %all-reduce.2.cloned.1.call-done = f32[512,512]{1,0:T(8,128)} async-done(((f32[512,512]{1,0:T(8,128)}), f32[512,512]{1,0:T(8,128)}) %all-reduce.2.cloned.1.call-update) | async-done | bytes 1048592 | tf_op jit(solution)/shard_map/while/body/eval_jaxpr/psum | solution.py:30
  1877.8 14.0 all-to-all-done
  1900.7 98.6 %all-reduce.2.cloned.1.call-done = f32[512,512]{1,0:T(8,128)} async-done(((f32[512,512]{1,0:T(8,128)}), f32[512,512]{1,0:T(8,128)}) %all-reduce.2.cloned.1.call-update) | async-done | bytes 1048592 | tf_op jit(solution)/shard_map/while/body/eval_jaxpr/psum | solution.py:30
  2034.8 98.2 %all-reduce.2.cloned.1.call-done = f32[512,512]{1,0:T(8,128)} async-done(((f32[512,512]{1,0:T(8,128)}), f32[512,512]{1,0:T(8,128)}) %all-reduce.2.cloned.1.call-update) | async-done | bytes 1048592 | tf_op jit(solution)/shard_map/while/body/eval_jaxpr/psum | solution.py:30
  (361 shorter events, 405.8 us)
Async XLA Ops:
  12.7 21.4 all-to-all-start
  18.1 120.9 %all-reduce.2.cloned.1.call-start = ((), (), s32[]{:S(2)}) async-start(), calls=%async_computation.1 | async-start | bytes 2097152 | tf_op jit(solution)/shard_map/while/body/eval_jaxpr/psum | solution.py:30
  145.4 20.4 all-to-all-start
  149.9 121.0 %all-reduce.2.cloned.1.call-start = ((), (), s32[]{:S(2)}) async-start(), calls=%async_computation.1 | async-start | bytes 2097152 | tf_op jit(solution)/shard_map/while/body/eval_jaxpr/psum | solution.py:30
  277.0 20.4 all-to-all-start
  281.4 122.0 %all-reduce.2.cloned.1.call-start = ((), (), s32[]{:S(2)}) async-start(), calls=%async_computation.1 | async-start | bytes 2097152 | tf_op jit(solution)/shard_map/while/body/eval_jaxpr/psum | solution.py:30
  409.6 20.4 all-to-all-start
  414.1 122.5 %all-reduce.2.cloned.1.call-start = ((), (), s32[]{:S(2)}) async-start(), calls=%async_computation.1 | async-start | bytes 2097152 | tf_op jit(solution)/shard_map/while/body/eval_jaxpr/psum | solution.py:30
  542.8 20.4 all-to-all-start
  547.2 121.3 %all-reduce.2.cloned.1.call-start = ((), (), s32[]{:S(2)}) async-start(), calls=%async_computation.1 | async-start | bytes 2097152 | tf_op jit(solution)/shard_map/while/body/eval_jaxpr/psum | solution.py:30
  674.6 20.4 all-to-all-start
  679.1 121.0 %all-reduce.2.cloned.1.call-start = ((), (), s32[]{:S(2)}) async-start(), calls=%async_computation.1 | async-start | bytes 2097152 | tf_op jit(solution)/shard_map/while/body/eval_jaxpr/psum | solution.py:30
  806.2 20.4 all-to-all-start
  810.7 122.2 %all-reduce.2.cloned.1.call-start = ((), (), s32[]{:S(2)}) async-start(), calls=%async_computation.1 | async-start | bytes 2097152 | tf_op jit(solution)/shard_map/while/body/eval_jaxpr/psum | solution.py:30
  939.0 20.4 all-to-all-start
  943.5 122.2 %all-reduce.2.cloned.1.call-start = ((), (), s32[]{:S(2)}) async-start(), calls=%async_computation.1 | async-start | bytes 2097152 | tf_op jit(solution)/shard_map/while/body/eval_jaxpr/psum | solution.py:30
  1071.8 20.4 all-to-all-start
  1076.3 121.9 %all-reduce.2.cloned.1.call-start = ((), (), s32[]{:S(2)}) async-start(), calls=%async_computation.1 | async-start | bytes 2097152 | tf_op jit(solution)/shard_map/while/body/eval_jaxpr/psum | solution.py:30
  1204.3 20.4 all-to-all-start
  1208.7 122.3 %all-reduce.2.cloned.1.call-start = ((), (), s32[]{:S(2)}) async-start(), calls=%async_computation.1 | async-start | bytes 2097152 | tf_op jit(solution)/shard_map/while/body/eval_jaxpr/psum | solution.py:30
  1337.2 20.4 all-to-all-start
  1341.7 123.7 %all-reduce.2.cloned.1.call-start = ((), (), s32[]{:S(2)}) async-start(), calls=%async_computation.1 | async-start | bytes 2097152 | tf_op jit(solution)/shard_map/while/body/eval_jaxpr/psum | solution.py:30
  1471.5 20.4 all-to-all-start
  1476.0 123.4 %all-reduce.2.cloned.1.call-start = ((), (), s32[]{:S(2)}) async-start(), calls=%async_computation.1 | async-start | bytes 2097152 | tf_op jit(solution)/shard_map/while/body/eval_jaxpr/psum | solution.py:30
  1605.6 20.4 all-to-all-start
  1610.0 122.5 %all-reduce.2.cloned.1.call-start = ((), (), s32[]{:S(2)}) async-start(), calls=%async_computation.1 | async-start | bytes 2097152 | tf_op jit(solution)/shard_map/while/body/eval_jaxpr/psum | solution.py:30
  1738.7 20.4 all-to-all-start
  1743.1 122.1 %all-reduce.2.cloned.1.call-start = ((), (), s32[]{:S(2)}) async-start(), calls=%async_computation.1 | async-start | bytes 2097152 | tf_op jit(solution)/shard_map/while/body/eval_jaxpr/psum | solution.py:30
  1871.4 20.4 all-to-all-start
  1875.8 123.5 %all-reduce.2.cloned.1.call-start = ((), (), s32[]{:S(2)}) async-start(), calls=%async_computation.1 | async-start | bytes 2097152 | tf_op jit(solution)/shard_map/while/body/eval_jaxpr/psum | solution.py:30
  2005.5 20.4 all-to-all-start
  2009.9 123.0 %all-reduce.2.cloned.1.call-start = ((), (), s32[]{:S(2)}) async-start(), calls=%async_computation.1 | async-start | bytes 2097152 | tf_op jit(solution)/shard_map/while/body/eval_jaxpr/psum | solution.py:30
  (18 other events, 26.3 us)
Sparse Core Ops, SparseCore 0:
  57.6 81.2 all-reduce.1
  174.8 95.9 all-reduce.1
  306.4 96.9 all-reduce.1
  439.0 97.4 all-reduce.1
  572.2 96.2 all-reduce.1
  704.1 95.9 all-reduce.1
  835.6 97.1 all-reduce.1
  968.5 97.1 all-reduce.1
  1101.2 96.8 all-reduce.1
  1233.7 97.2 all-reduce.1
  1366.6 98.6 all-reduce.1
  1501.0 98.4 all-reduce.1
  1635.0 97.4 all-reduce.1
  1768.1 97.0 all-reduce.1
  1900.8 98.4 all-reduce.1
  2034.9 97.9 all-reduce.1
where the time goes:
time: 2150 us; the launch traced here: 2140 us
  waiting for transfers between devices  1770 us (82%)
  local copies, waits for them, and re-layouts  153 us (7%)
  starting transfers between devices  72.4 us (3%)
  other arithmetic  70.8 us (3%)
  matrix products  64.5 us (3%)
    psum x16, waiting for transfers between devices, from_root(): return lax.psum(block, axis)  1540 us
    all_to_all x16, waiting for transfers between devices, sent_to_all(): lax.all_to_all(jnp.broadcast_to(array[None], (length, *array.shape)), axi...  225 us
    all_to_all x16, starting transfers between devices, sent_to_all(): lax.all_to_all(jnp.broadcast_to(array[None], (length, *array.shape)), axi...  71.8 us
    dot_general x21, matrix products, dot_high(): jnp.dot(left, right, precision=lax.Precision.HIGHEST, preferred_element_t...  64.5 us
  transfers between devices with their start and end apart: 32, of which 32 were waited for; matrix products, arithmetic and copies ran while one was open for 1% of the time, Pallas kernels for 0%

commit v1 on v0

--- a/solution.py
+++ b/solution.py
@@ -27,7 +27,7 @@
 
 def from_root(block, axis, source):
     block = jnp.where(lax.axis_index(axis) == source, block, jnp.zeros_like(block))
-    return lax.psum(block, axis)
+    return jnp.sum(lax.all_gather(block, axis), axis=0)
 
 
 def dot_high(left, right):

time: 2150 us -> 2690 us (1.25)
  waiting for transfers between devices: 1770 us -> 2170 us
  other arithmetic: 70.8 us -> 213 us
    all_gather x0 -> x16, waiting for transfers between devices: none -> 1940 us  [from_root(): return jnp.sum(lax.all_gather(block, axis), axis=0)]
    psum x16 -> x0, waiting for transfers between devices: 1540 us -> none  [from_root(): return lax.psum(block, axis)]
    reduce_sum x0 -> x16, other arithmetic: none -> 142 us  [from_root(): return jnp.sum(lax.all_gather(block, axis), axis=0)]
where the time goes in v1:
time: 2690 us; the launch traced here: 2680 us
  waiting for transfers between devices  2170 us (81%)
  other arithmetic  213 us (8%)
  local copies, waits for them, and re-layouts  153 us (6%)
  starting transfers between devices  72.3 us (3%)
  matrix products  64.5 us (2%)
    all_gather x16, waiting for transfers between devices, from_root(): return jnp.sum(lax.all_gather(block, axis), axis=0)  1940 us
    all_to_all x16, waiting for transfers between devices, sent_to_all(): lax.all_to_all(jnp.broadcast_to(array[None], (length, *array.shape)), axi...  225 us
    reduce_sum x16, other arithmetic, from_root(): return jnp.sum(lax.all_gather(block, axis), axis=0)  142 us
    all_to_all x16, starting transfers between devices, sent_to_all(): lax.all_to_all(jnp.broadcast_to(array[None], (length, *array.shape)), axi...  71.8 us
    dot_general x21, matrix products, dot_high(): jnp.dot(left, right, precision=lax.Precision.HIGHEST, preferred_element_t...  64.5 us
  transfers between devices with their start and end apart: 32, of which 32 were waited for; matrix products, arithmetic and copies ran while one was open for 1% of the time, Pallas kernels for 0%

profile of v1, /device:TPU:0, one launch (start us, length us, event | category | flops | bytes accessed | tf_op | source)
XLA Modules:
  0.0 2684.5 jit_solution(3608957134663954694)
XLA Ops:
  10.7 2667.3 %while.17 = (s32[]{:T(128)}, f32[24,64,512]{2,1,0:T(8,128)}, s32[]{:T(128)}, s32[16,512]{1,0:T(8,128)}, s32[]{:T(128)}, /*index=5*/f32[512,512]{1,0:T(8,128)S(1)...) while((s32[]{:T(128)}, f32[24,64,512]{2,1,0:T(8,128)}, ...), condition=%wide.region_6.7_spmd.clone.clone, body=%wide.region_0.6_spmd.clone.clone.sunk | while | flops 9670760448 | bytes 120211424 | solution.py:75
  20.0 14.0 all-to-all-done
  57.5 105.8 %all-gather.6.cloned.1.call-done = f32[8192,512]{1,0:T(8,128)} async-done(((f32[512,512]{1,0:T(8,128)}), f32[8192,512]{1,0:T(8,128)}) %all-gather.6.cloned.1.call-update) | async-done | bytes 16777232 | tf_op jit(solution)/shard_map/while/body/eval_jaxpr/all_gather | solution.py:30
  185.0 14.0 all-to-all-done
  208.0 120.9 %all-gather.6.cloned.1.call-done = f32[8192,512]{1,0:T(8,128)} async-done(((f32[512,512]{1,0:T(8,128)}), f32[8192,512]{1,0:T(8,128)}) %all-gather.6.cloned.1.call-update) | async-done | bytes 16777232 | tf_op jit(solution)/shard_map/while/body/eval_jaxpr/all_gather | solution.py:30
  350.3 14.0 all-to-all-done
  373.2 122.7 %all-gather.6.cloned.1.call-done = f32[8192,512]{1,0:T(8,128)} async-done(((f32[512,512]{1,0:T(8,128)}), f32[8192,512]{1,0:T(8,128)}) %all-gather.6.cloned.1.call-update) | async-done | bytes 16777232 | tf_op jit(solution)/shard_map/while/body/eval_jaxpr/all_gather | solution.py:30
  517.4 14.0 all-to-all-done
  540.3 122.4 %all-gather.6.cloned.1.call-done = f32[8192,512]{1,0:T(8,128)} async-done(((f32[512,512]{1,0:T(8,128)}), f32[8192,512]{1,0:T(8,128)}) %all-gather.6.cloned.1.call-update) | async-done | bytes 16777232 | tf_op jit(solution)/shard_map/while/body/eval_jaxpr/all_gather | solution.py:30
  684.2 14.0 all-to-all-done
  707.1 121.2 %all-gather.6.cloned.1.call-done = f32[8192,512]{1,0:T(8,128)} async-done(((f32[512,512]{1,0:T(8,128)}), f32[8192,512]{1,0:T(8,128)}) %all-gather.6.cloned.1.call-update) | async-done | bytes 16777232 | tf_op jit(solution)/shard_map/while/body/eval_jaxpr/all_gather | solution.py:30
  849.8 14.0 all-to-all-done
  872.7 120.9 %all-gather.6.cloned.1.call-done = f32[8192,512]{1,0:T(8,128)} async-done(((f32[512,512]{1,0:T(8,128)}), f32[8192,512]{1,0:T(8,128)}) %all-gather.6.cloned.1.call-update) | async-done | bytes 16777232 | tf_op jit(solution)/shard_map/while/body/eval_jaxpr/all_gather | solution.py:30
  1015.1 14.0 all-to-all-done
  1038.0 122.4 %all-gather.6.cloned.1.call-done = f32[8192,512]{1,0:T(8,128)} async-done(((f32[512,512]{1,0:T(8,128)}), f32[8192,512]{1,0:T(8,128)}) %all-gather.6.cloned.1.call-update) | async-done | bytes 16777232 | tf_op jit(solution)/shard_map/while/body/eval_jaxpr/all_gather | solution.py:30
  1181.9 14.0 all-to-all-done
  1204.8 122.2 %all-gather.6.cloned.1.call-done = f32[8192,512]{1,0:T(8,128)} async-done(((f32[512,512]{1,0:T(8,128)}), f32[8192,512]{1,0:T(8,128)}) %all-gather.6.cloned.1.call-update) | async-done | bytes 16777232 | tf_op jit(solution)/shard_map/while/body/eval_jaxpr/all_gather | solution.py:30
  1348.4 14.0 all-to-all-done
  1371.3 122.8 %all-gather.6.cloned.1.call-done = f32[8192,512]{1,0:T(8,128)} async-done(((f32[512,512]{1,0:T(8,128)}), f32[8192,512]{1,0:T(8,128)}) %all-gather.6.cloned.1.call-update) | async-done | bytes 16777232 | tf_op jit(solution)/shard_map/while/body/eval_jaxpr/all_gather | solution.py:30
  1515.5 14.0 all-to-all-done
  1538.4 122.4 %all-gather.6.cloned.1.call-done = f32[8192,512]{1,0:T(8,128)} async-done(((f32[512,512]{1,0:T(8,128)}), f32[8192,512]{1,0:T(8,128)}) %all-gather.6.cloned.1.call-update) | async-done | bytes 16777232 | tf_op jit(solution)/shard_map/while/body/eval_jaxpr/all_gather | solution.py:30
  1682.3 14.0 all-to-all-done
  1705.2 123.7 %all-gather.6.cloned.1.call-done = f32[8192,512]{1,0:T(8,128)} async-done(((f32[512,512]{1,0:T(8,128)}), f32[8192,512]{1,0:T(8,128)}) %all-gather.6.cloned.1.call-update) | async-done | bytes 16777232 | tf_op jit(solution)/shard_map/while/body/eval_jaxpr/all_gather | solution.py:30
  1850.3 14.0 all-to-all-done
  1873.3 123.4 %all-gather.6.cloned.1.call-done = f32[8192,512]{1,0:T(8,128)} async-done(((f32[512,512]{1,0:T(8,128)}), f32[8192,512]{1,0:T(8,128)}) %all-gather.6.cloned.1.call-update) | async-done | bytes 16777232 | tf_op jit(solution)/shard_map/while/body/eval_jaxpr/all_gather | solution.py:30
  2018.1 14.0 all-to-all-done
  2041.0 122.5 %all-gather.6.cloned.1.call-done = f32[8192,512]{1,0:T(8,128)} async-done(((f32[512,512]{1,0:T(8,128)}), f32[8192,512]{1,0:T(8,128)}) %all-gather.6.cloned.1.call-update) | async-done | bytes 16777232 | tf_op jit(solution)/shard_map/while/body/eval_jaxpr/all_gather | solution.py:30
  2184.9 14.0 all-to-all-done
  2207.9 122.2 %all-gather.6.cloned.1.call-done = f32[8192,512]{1,0:T(8,128)} async-done(((f32[512,512]{1,0:T(8,128)}), f32[8192,512]{1,0:T(8,128)}) %all-gather.6.cloned.1.call-update) | async-done | bytes 16777232 | tf_op jit(solution)/shard_map/while/body/eval_jaxpr/all_gather | solution.py:30
  2374.4 123.4 %all-gather.6.cloned.1.call-done = f32[8192,512]{1,0:T(8,128)} async-done(((f32[512,512]{1,0:T(8,128)}), f32[8192,512]{1,0:T(8,128)}) %all-gather.6.cloned.1.call-update) | async-done | bytes 16777232 | tf_op jit(solution)/shard_map/while/body/eval_jaxpr/all_gather | solution.py:30
  2519.2 14.0 all-to-all-done
  2542.1 122.8 %all-gather.6.cloned.1.call-done = f32[8192,512]{1,0:T(8,128)} async-done(((f32[512,512]{1,0:T(8,128)}), f32[8192,512]{1,0:T(8,128)}) %all-gather.6.cloned.1.call-update) | async-done | bytes 16777232 | tf_op jit(solution)/shard_map/while/body/eval_jaxpr/all_gather | solution.py:30
  (377 shorter events, 548.2 us)
Async XLA Ops:
  12.7 21.4 all-to-all-start
  18.1 145.2 %all-gather.6.cloned.1.call-start = ((), (), s32[]{:S(2)}) async-start(), calls=%async_computation.1 | async-start | bytes 17825792 | tf_op jit(solution)/shard_map/while/body/eval_jaxpr/all_gather | solution.py:30
  178.7 20.4 all-to-all-start
  183.1 145.8 %all-gather.6.cloned.1.call-start = ((), (), s32[]{:S(2)}) async-start(), calls=%async_computation.1 | async-start | bytes 17825792 | tf_op jit(solution)/shard_map/while/body/eval_jaxpr/all_gather | solution.py:30
  344.0 20.4 all-to-all-start
  348.4 147.6 %all-gather.6.cloned.1.call-start = ((), (), s32[]{:S(2)}) async-start(), calls=%async_computation.1 | async-start | bytes 17825792 | tf_op jit(solution)/shard_map/while/body/eval_jaxpr/all_gather | solution.py:30
  511.0 20.4 all-to-all-start
  515.5 147.3 %all-gather.6.cloned.1.call-start = ((), (), s32[]{:S(2)}) async-start(), calls=%async_computation.1 | async-start | bytes 17825792 | tf_op jit(solution)/shard_map/while/body/eval_jaxpr/all_gather | solution.py:30
  677.9 20.4 all-to-all-start
  682.3 146.1 %all-gather.6.cloned.1.call-start = ((), (), s32[]{:S(2)}) async-start(), calls=%async_computation.1 | async-start | bytes 17825792 | tf_op jit(solution)/shard_map/while/body/eval_jaxpr/all_gather | solution.py:30
  843.4 20.4 all-to-all-start
  847.9 145.8 %all-gather.6.cloned.1.call-start = ((), (), s32[]{:S(2)}) async-start(), calls=%async_computation.1 | async-start | bytes 17825792 | tf_op jit(solution)/shard_map/while/body/eval_jaxpr/all_gather | solution.py:30
  1008.7 20.4 all-to-all-start
  1013.2 147.3 %all-gather.6.cloned.1.call-start = ((), (), s32[]{:S(2)}) async-start(), calls=%async_computation.1 | async-start | bytes 17825792 | tf_op jit(solution)/shard_map/while/body/eval_jaxpr/all_gather | solution.py:30
  1175.5 20.4 all-to-all-start
  1180.0 147.0 %all-gather.6.cloned.1.call-start = ((), (), s32[]{:S(2)}) async-start(), calls=%async_computation.1 | async-start | bytes 17825792 | tf_op jit(solution)/shard_map/while/body/eval_jaxpr/all_gather | solution.py:30
  1342.0 20.4 all-to-all-start
  1346.5 147.6 %all-gather.6.cloned.1.call-start = ((), (), s32[]{:S(2)}) async-start(), calls=%async_computation.1 | async-start | bytes 17825792 | tf_op jit(solution)/shard_map/while/body/eval_jaxpr/all_gather | solution.py:30
  1509.2 20.4 all-to-all-start
  1513.6 147.3 %all-gather.6.cloned.1.call-start = ((), (), s32[]{:S(2)}) async-start(), calls=%async_computation.1 | async-start | bytes 17825792 | tf_op jit(solution)/shard_map/while/body/eval_jaxpr/all_gather | solution.py:30
  1675.9 20.4 all-to-all-start
  1680.4 148.5 %all-gather.6.cloned.1.call-start = ((), (), s32[]{:S(2)}) async-start(), calls=%async_computation.1 | async-start | bytes 17825792 | tf_op jit(solution)/shard_map/while/body/eval_jaxpr/all_gather | solution.py:30
  1844.0 20.4 all-to-all-start
  1848.4 148.3 %all-gather.6.cloned.1.call-start = ((), (), s32[]{:S(2)}) async-start(), calls=%async_computation.1 | async-start | bytes 17825792 | tf_op jit(solution)/shard_map/while/body/eval_jaxpr/all_gather | solution.py:30
  2011.7 20.4 all-to-all-start
  2016.2 147.3 %all-gather.6.cloned.1.call-start = ((), (), s32[]{:S(2)}) async-start(), calls=%async_computation.1 | async-start | bytes 17825792 | tf_op jit(solution)/shard_map/while/body/eval_jaxpr/all_gather | solution.py:30
  2178.6 20.4 all-to-all-start
  2183.0 147.0 %all-gather.6.cloned.1.call-start = ((), (), s32[]{:S(2)}) async-start(), calls=%async_computation.1 | async-start | bytes 17825792 | tf_op jit(solution)/shard_map/while/body/eval_jaxpr/all_gather | solution.py:30
  2345.1 20.4 all-to-all-start
  2349.5 148.2 %all-gather.6.cloned.1.call-start = ((), (), s32[]{:S(2)}) async-start(), calls=%async_computation.1 | async-start | bytes 17825792 | tf_op jit(solution)/shard_map/while/body/eval_jaxpr/all_gather | solution.py:30
  2512.8 20.4 all-to-all-start
  2517.3 147.6 %all-gather.6.cloned.1.call-start = ((), (), s32[]{:S(2)}) async-start(), calls=%async_computation.1 | async-start | bytes 17825792 | tf_op jit(solution)/shard_map/while/body/eval_jaxpr/all_gather | solution.py:30
  (18 other events, 26.3 us)
Sparse Core Ops, SparseCore 0:
  57.6 105.6 all-gather.5
  208.1 120.7 all-gather.5
  373.4 122.5 all-gather.5
  540.4 122.2 all-gather.5
  707.3 121.0 all-gather.5
  872.8 120.7 all-gather.5
  1038.1 122.2 all-gather.5
  1204.9 121.9 all-gather.5
  1371.4 122.5 all-gather.5
  1538.6 122.2 all-gather.5
  1705.3 123.5 all-gather.5
  1873.4 123.2 all-gather.5
  2041.1 122.3 all-gather.5
  2208.0 122.0 all-gather.5
  2374.5 123.2 all-gather.5
  2542.2 122.6 all-gather.5
